TPU v7x, 256 devices: a whole 4x4x8 slice. The times are simulated.
256 devices in a mesh: cuts: 16 (over z, core), rank: 16 (over x, y).
Axes of the slice: x: 4, y: 4, z: 8, core: 2. Of those that a mesh axis runs over, the one named last changes fastest.
Arguments:
- core_one: float32 [512, 320, 512], P('rank', 'cuts'), may hold values from -6 to 6
- core_two: float32 [512, 320, 512], P('rank', 'cuts'), may hold values from -0.25 to 0.25
- right_sketch: float32 [512, 128], replicated, may hold values from -0.25 to 0.25
- sketch_core: float32 [128, 320, 128], P(None, 'cuts'), may hold values from -0.03125 to 0.03125
Outputs:
- left_core: float32 [512, 320, 128], P('rank', 'cuts')
- middle_core: float32 [128, 320, 128], P('rank', 'cuts')
- carry: float32 [128, 512], replicated
All inputs are finite; a program needn't handle non-finite values.
Results may differ from a plain program's by a relative error of at most 0.00015.
Values sent between devices are 32-bit elements; how exact they have to be, the bound alone decides.
A program may use at most 64 MiB of HBM per device.

v0:
```python
import functools
import math

import jax
import jax.numpy as jnp
from jax import lax
from jax.experimental import pallas as pl
from jax.experimental.pallas import tpu as pltpu
from jax.sharding import PartitionSpec as P

MESH = pl.DeviceIdType.MESH
F32 = jnp.float32
BF16 = jnp.bfloat16
NN = (((1,), (0,)), ((), ()))
NT = (((1,), (1,)), ((), ()))
TN = (((0,), (0,)), ((), ()))


def split(value):
    high = value.astype(BF16)
    return high, (value - high.astype(F32)).astype(BF16)


def product(left, right, dims):
    (left_high, left_low), (right_high, right_low) = left, right
    dot = functools.partial(lax.dot_general, dimension_numbers=dims, preferred_element_type=F32)
    return dot(left_high, right_high) + (dot(left_high, right_low) + dot(left_low, right_high))


def exact(left, right, dims):
    return lax.dot_general(
        left, right, dims, precision=lax.Precision.HIGHEST, preferred_element_type=F32
    )


def inverse_factor(gram_ref, width):
    blocks = width // 8
    lane = lax.broadcasted_iota(jnp.int32, (8, width), 1)
    row = lax.broadcasted_iota(jnp.int32, (8, width), 0)
    unit = (lane == row).astype(F32)
    block_of = lax.broadcasted_iota(jnp.int32, (blocks, 8, width), 0)
    first_lanes = lax.broadcasted_iota(jnp.int32, (blocks, 8, width), 2) < 8

    def spread(value, i):
        return jnp.broadcast_to(value[i : i + 1, :], (8, width))

    def step(block, carry):
        start = pl.multiple_of(block * 8, 8)
        own = gram_ref[pl.ds(start, 8), :]
        column = [jnp.broadcast_to(own[:, m : m + 1], (8, width)) for m in range(8)]
        entry = [[spread(column[m], i) if m <= i else None for m in range(8)] for i in range(8)]
        replaced = jnp.where(lane < 8, unit, own)
        rows = [spread(replaced, i) for i in range(8)]
        inverse, solved = [], []
        for j in range(8):
            inverse.append(lax.rsqrt(entry[j][j]))
            solved.append(rows[j] * inverse[j])
            for i in range(j + 1, 8):
                entry[i][j] = entry[i][j] * inverse[j]
            for i in range(j + 1, 8):
                rows[i] = rows[i] - entry[i][j] * solved[j]
                for m in range(j + 1, i + 1):
                    entry[i][m] = entry[i][m] - entry[i][j] * entry[m][j]
        back = list(solved)
        for j in reversed(range(8)):
            for i in range(j + 1, 8):
                back[j] = back[j] - entry[i][j] * back[i]
            back[j] = back[j] * inverse[j]
        done = solved[0]
        for j in range(1, 8):
            done = jnp.where(row == j, solved[j], done)
        whole = gram_ref[...].reshape(blocks, 8, width)
        update = jnp.where(first_lanes, 0.0, whole)
        for m in range(8):
            update = update - whole[:, :, m : m + 1] * back[m][None]
        whole = jnp.where(block_of > block, update, jnp.where(block_of == block, done[None], whole))
        gram_ref[...] = pltpu.roll(whole.reshape(width, width), width - 8, 1)
        return carry

    lax.fori_loop(0, blocks, step, 0)
    lower = lax.broadcasted_iota(jnp.int32, (width, width), 0) >= lax.broadcasted_iota(
        jnp.int32, (width, width), 1
    )
    gram_ref[...] = jnp.where(lower, gram_ref[...], 0.0)


def kernel(
    n_cuts, n_rank, scale_left, scale_middle,
    one_ref, two_ref, sketch_ref, core_ref, left_ref, middle_ref, carry_ref,
    one_high, one_low, bridge_part, bridge_recv, bridge,
    first_rows, full_two, projected, second_rows, returned, gram,
    reduce_part, reduce_recv, reduce_sum, gather_recv, gather_sum, reduced,
    send_sem, recv_sem, two_send, two_recv, back_send, back_recv,
):
    slices, local, width = one_ref.shape
    out_width = sketch_ref.shape[1]
    band = out_width // n_rank
    chunk = out_width // n_cuts
    my_cut, my_rank = lax.axis_index("cuts"), lax.axis_index("rank")
    full, extra = slices // n_rank, slices % n_rank
    stride = max((n_rank - 1) // (extra - 1), 1) if extra > 1 else 1
    slots = full + (1 if extra else 0)

    def owner(n):
        return n % n_rank if n < full * n_rank else (n - full * n_rank) * stride

    def has_extra(rank):
        return jnp.logical_and(lax.rem(rank, stride) == 0, lax.div(rank, stride) < extra)

    def cut_device(k):
        peer = lax.rem(my_cut + k, n_cuts)
        return peer, (peer, my_rank)

    def rank_device(k):
        peer = lax.rem(my_rank + k, n_rank)
        return peer, (my_cut, peer)

    def remote(source, target, send, recv, device):
        return pltpu.make_async_remote_copy(
            src_ref=source, dst_ref=target, send_sem=send, recv_sem=recv,
            device_id=device, device_id_type=MESH,
        )

    def each(count, body):
        def step(k, carry):
            body(k)
            return carry
        lax.fori_loop(1, count, step, 0)

    def rows_of(index, size):
        return pl.ds(pl.multiple_of(index * size, size), size)

    barrier = pltpu.get_barrier_semaphore()

    def greet(device_of):
        def body(k):
            pl.semaphore_signal(barrier, inc=1, device_id=device_of(k)[1], device_id_type=MESH)
        return body

    each(n_cuts, greet(cut_device))
    each(n_rank, greet(rank_device))

    sketch_parts = split(sketch_ref[...])
    sketched = product(split(two_ref[...].reshape(slices * local, width)), sketch_parts, NN)
    lanes = jnp.concatenate([sketched[n * local : (n + 1) * local] for n in range(slices)], axis=1)
    weights = jnp.concatenate([core_ref[n] for n in range(slices)], axis=1)
    bridge_part[...] = product(split(lanes), split(weights), NT)
    bridge_recv[my_cut] = bridge_part[...]

    pl.semaphore_wait(barrier, n_cuts + n_rank - 2)

    def exchange(source_of, target, phase, device_of, count):
        def body(k):
            peer, device = device_of(k)
            remote(source_of(peer), target, send_sem.at[phase, peer],
                   recv_sem.at[phase, my_cut if device_of is cut_device else my_rank], device).start()
        each(count, body)

    def arrive(target_of, phase, device_of, count):
        def body(k):
            peer, device = device_of(k)
            remote(target_of(peer), target_of(peer), send_sem.at[phase, peer], recv_sem.at[phase, peer], device).wait_recv()
        each(count, body)

    def drain(source, phase, device_of, count):
        def body(k):
            peer, device = device_of(k)
            remote(source, source, send_sem.at[phase, peer], recv_sem.at[phase, peer], device).wait_send()
        each(count, body)

    def total(ref, count):
        value = ref[0]
        for k in range(1, count):
            value = value + ref[k]
        return value

    exchange(lambda peer: bridge_part, bridge_recv.at[my_cut], 0, cut_device, n_cuts)

    one_high[...], one_low[...] = split(one_ref[...].reshape(slices * local, width))
    arrive(lambda peer: bridge_recv.at[peer], 0, cut_device, n_cuts)
    own_bridge = bridge.at[rows_of(my_rank, local), :]
    own_bridge[...] = total(bridge_recv, n_cuts)
    exchange(lambda peer: own_bridge, own_bridge, 1, rank_device, n_rank)
    arrive(lambda peer: bridge.at[rows_of(peer, local), :], 1, rank_device, n_rank)

    own_rows = rows_of(my_rank, local)

    def send_two(n, slot, target_rank):
        @pl.when(my_rank != target_rank)
        def _():
            remote(two_ref.at[n], full_two.at[slot, own_rows, :], two_send.at[n],
                   two_recv.at[slot, my_rank], (my_cut, target_rank)).start()

        @pl.when(my_rank == target_rank)
        def _():
            full_two[slot, own_rows, :] = two_ref[n]

    for slot in range(full):
        def body(k, carry):
            peer, _ = rank_device(k)
            send_two(slot * n_rank + peer, slot, peer)
            return carry
        lax.fori_loop(0, n_rank, body, 0)
    for n in range(full * n_rank, slices):
        send_two(n, full, owner(n))

    def stage(rows_bf, matrix_parts, bridge_ref, index, between):
        base = 2 + 3 * index
        part, recv1, sum1, recv2, sum2, whole = (
            reduce_part.at[index], reduce_recv.at[index], reduce_sum.at[index],
            gather_recv.at[index], gather_sum.at[index], reduced.at[index],
        )
        part[...] = product(rows_bf, matrix_parts, TN)
        recv1[my_cut] = part[rows_of(my_cut, chunk), :]
        exchange(lambda peer: part.at[rows_of(peer, chunk), :], recv1.at[my_cut], base, cut_device, n_cuts)
        between[0]()
        arrive(lambda peer: recv1.at[peer], base, cut_device, n_cuts)
        sum1[...] = total(recv1, n_cuts)
        recv2[my_rank] = sum1[...]
        exchange(lambda peer: sum1, recv2.at[my_rank], base + 1, rank_device, n_rank)
        between[1]()
        arrive(lambda peer: recv2.at[peer], base + 1, rank_device, n_rank)
        own = whole.at[rows_of(my_cut, chunk), :]
        own[...] = total(recv2, n_rank)
        exchange(lambda peer: own, own, base + 2, cut_device, n_cuts)
        between[2]()
        arrive(lambda peer: whole.at[rows_of(peer, chunk), :], base + 2, cut_device, n_cuts)
        gram[...] = exact(whole[...], bridge_ref[...], NN)
        inverse_factor(gram, out_width)

    def nothing():
        pass

    one_parts = (one_high[...], one_low[...])
    first_rows[...] = product(one_parts, split(bridge[...]), NN)

    def land_two():
        for slot in range(slots):
            def wait_rows():
                def body(k):
                    peer, device = rank_device(k)
                    place = full_two.at[slot, rows_of(peer, local), :]
                    remote(place, place, two_send.at[0], two_recv.at[slot, peer], device).wait_recv()
                each(n_rank, body)
            if slot < full:
                wait_rows()
            else:
                pl.when(has_extra(my_rank))(wait_rows)

    stage(split(first_rows[...]), (one_high[...], one_low[...]), bridge, 0, (nothing, nothing, land_two))
    first_carry = split(exact(gram[...], reduced[0], NN))
    first_inverse = split(gram[...] * scale_left)

    for slot in range(slots):
        def project():
            here = slice(slot * out_width, (slot + 1) * out_width)
            block = product(first_carry, split(full_two[slot]), NN)
            projected[here, :] = block
            second_rows[here, :] = product(split(block), sketch_parts, NN)

        def blank():
            here = slice(slot * out_width, (slot + 1) * out_width)
            projected[here, :] = jnp.zeros((out_width, width), F32)
            second_rows[here, :] = jnp.zeros((out_width, out_width), F32)

        if slot < full:
            project()
        else:
            pl.when(has_extra(my_rank))(project)
            pl.when(jnp.logical_not(has_extra(my_rank)))(blank)

    def give_back():
        for slot in range(slots):
            n = slot * n_rank + (my_rank if slot < full else lax.div(my_rank, stride))

            def send_rows():
                returned[n] = second_rows[pl.ds(pl.multiple_of(slot * out_width + my_rank * band, 8), band), :]

                def body(k):
                    peer, device = rank_device(k)
                    source = second_rows.at[pl.ds(pl.multiple_of(slot * out_width + peer * band, 8), band), :]
                    remote(source, returned.at[n], back_send.at[slot, peer], back_recv.at[n], device).start()
                each(n_rank, body)
            if slot < full:
                send_rows()
            else:
                pl.when(has_extra(my_rank))(send_rows)

    def finish_left():
        ortho = product(split(first_rows[...]), first_inverse, NT)
        left_ref[...] = ortho.reshape(slices, local, out_width)

    def land_back():
        for n in range(slices):
            @pl.when(my_rank != owner(n))
            def _():
                remote(returned.at[n], returned.at[n], back_send.at[0, 0], back_recv.at[n],
                       (my_cut, my_rank)).wait_recv()

    stage(split(second_rows[...]), split(projected[...]), sketch_ref, 1, (give_back, finish_left, land_back))
    carry_ref[...] = exact(gram[...], reduced[1], NN)
    flat = returned[...].reshape(slices * band, out_width)
    middle = product(split(flat), split(gram[...] * scale_middle), NT)
    middle_ref[...] = middle.reshape(slices, band, out_width)

    drain(bridge_part, 0, cut_device, n_cuts)
    drain(own_bridge, 1, rank_device, n_rank)
    for index in range(2):
        piece = reduce_sum.at[index]
        drain(piece, 2 + 3 * index, cut_device, n_cuts)
        drain(piece, 3 + 3 * index, rank_device, n_rank)
        drain(piece, 4 + 3 * index, cut_device, n_cuts)
    for n in range(slices):
        @pl.when(my_rank != owner(n))
        def _():
            remote(two_ref.at[n], two_ref.at[n], two_send.at[n], two_recv.at[0, 0], (my_cut, my_rank)).wait_send()
    for slot in range(slots):
        def sent():
            def body(k):
                peer, device = rank_device(k)
                remote(returned.at[0], returned.at[0], back_send.at[slot, peer], back_recv.at[0], device).wait_send()
            each(n_rank, body)
        if slot < full:
            sent()
        else:
            pl.when(has_extra(my_rank))(sent)


def solution(mesh):
    n_cuts, n_rank = mesh.shape["cuts"], mesh.shape["rank"]

    def on_device(core_one, core_two, right_sketch, sketch_core):
        local, slices, width = core_one.shape
        out_width = right_sketch.shape[1]
        band, chunk = out_width // n_rank, out_width // n_cuts
        slots = -(-slices // n_rank)
        rows = local * slices
        scale_left = math.sqrt(local * n_rank * slices * n_cuts)
        scale_middle = math.sqrt(out_width * slices * n_cuts)
        vmem, sems = pltpu.VMEM, pltpu.SemaphoreType.DMA
        widest = max(n_cuts, n_rank)
        left, middle, carry = pl.pallas_call(
            functools.partial(kernel, n_cuts, n_rank, scale_left, scale_middle),
            out_shape=(
                jax.ShapeDtypeStruct((slices, local, out_width), F32),
                jax.ShapeDtypeStruct((slices, band, out_width), F32),
                jax.ShapeDtypeStruct((out_width, width), F32),
            ),
            in_specs=[pl.BlockSpec(memory_space=pltpu.VMEM)] * 4,
            out_specs=(pl.BlockSpec(memory_space=pltpu.VMEM),) * 3,
            scratch_shapes=[
                vmem((rows, width), BF16),
                vmem((rows, width), BF16),
                vmem((local, out_width), F32),
                vmem((n_cuts, local, out_width), F32),
                vmem((width, out_width), F32),
                vmem((rows, out_width), F32),
                vmem((slots, width, width), F32),
                vmem((slots * out_width, width), F32),
                vmem((slots * out_width, out_width), F32),
                vmem((slices, band, out_width), F32),
                vmem((out_width, out_width), F32),
                vmem((2, out_width, width), F32),
                vmem((2, n_cuts, chunk, width), F32),
                vmem((2, chunk, width), F32),
                vmem((2, n_rank, chunk, width), F32),
                vmem((2, chunk, width), F32),
                vmem((2, out_width, width), F32),
                sems((8, widest)),
                sems((8, widest)),
                sems((slices,)),
                sems((slots, n_rank)),
                sems((slots, n_rank)),
                sems((slices,)),
            ],
            compiler_params=pltpu.CompilerParams(
                collective_id=0, has_side_effects=True, vmem_limit_bytes=60 * 1024 * 1024
            ),
        )(
            core_one.transpose(1, 0, 2), core_two.transpose(1, 0, 2),
            right_sketch, sketch_core.transpose(1, 0, 2),
        )
        return left.transpose(1, 0, 2), middle.transpose(1, 0, 2), carry

    placed = (P("rank", "cuts", None), P("rank", "cuts", None), P(), P(None, "cuts", None))
    return jax.shard_map(
        on_device,
        mesh=mesh,
        in_specs=placed,
        out_specs=(P("rank", "cuts", None), P("rank", "cuts", None), P()),
        check_vma=False,
    )
```

profile of v0, /device:TPU:1, one launch (start us, length us, event | category | flops | bytes accessed | tf_op | source)
XLA Modules:
  0.0 109.9 jit_solution(13995018870560302958)
XLA Ops:
  0.6 104.3 %shard_map.67 = (f32[20,32,128]{2,1,0:T(8,128)}, f32[20,8,128]{2,1,0:T(8,128)}, f32[128,512]{1,0:T(8,128)}) custom-call(f32[20,32,512]{2,1,0:T(8,128)} %bitcast.5, f32[20,32,512]{2,1,0:T(8,128)} %bitcast.6, f32[512,128]{1,0:T(8,128)} %sketch_ref.1, f32[20,128,128]{2,1,0:T(8,128)} %bitcast.7), custom_call_target="tpu_custom_call" | custom-call | tf_op jit(solution)/shard_map/pallas_call | solution.py:342
  105.0 1.7 %copy.10 = f32[32,20,128]{2,0,1:T(8,128)} copy(f32[32,20,128]{2,0,1:T(8,128)} %bitcast.8) | data formatting | bytes 655360
  106.7 1.5 %copy.11 = f32[8,20,128]{2,0,1:T(8,128)} copy(f32[8,20,128]{2,0,1:T(8,128)} %bitcast.9) | data formatting | bytes 163840
  108.2 1.7 %copy.12 = f32[128,512]{1,0:T(8,128)} copy(f32[128,512]{1,0:T(8,128)} %get-tuple-element.14) | data formatting | bytes 524288
where the time goes:
time: 110 us
  Pallas kernels  104 us (95%)
  local copies, waits for them, and re-layouts  4.91 us (4%)
    pallas_call x1, Pallas kernels, on_device(): pl.pallas_call(functools.partial(kernel, n_cuts, n_rank, scale_left, scal...  104 us
    unnamed x3, local copies, waits for them, and re-layouts  4.91 us

commit v1 on v0

v1 whole, which is shorter than its diff:
```python
import functools
import math

import jax
import jax.numpy as jnp
from jax import lax
from jax.experimental import pallas as pl
from jax.experimental.pallas import tpu as pltpu
from jax.sharding import PartitionSpec as P

MESH = pl.DeviceIdType.MESH
F32 = jnp.float32
BF16 = jnp.bfloat16
NN = (((1,), (0,)), ((), ()))
NT = (((1,), (1,)), ((), ()))
TN = (((0,), (0,)), ((), ()))
PIECES = (0.25, 0.5, 0.7)
EXTRA_PIECE = 3


def split(value):
    high = value.astype(BF16)
    return high, (value - high.astype(F32)).astype(BF16)


def product(left, right, dims):
    (left_high, left_low), (right_high, right_low) = left, right
    dot = functools.partial(lax.dot_general, dimension_numbers=dims, preferred_element_type=F32)
    return dot(left_high, right_high) + (dot(left_high, right_low) + dot(left_low, right_high))


def exact(left, right, dims):
    return lax.dot_general(
        left, right, dims, precision=lax.Precision.HIGHEST, preferred_element_type=F32
    )


def inverse_factor(gram_ref, width):
    blocks = width // 8
    lane = lax.broadcasted_iota(jnp.int32, (8, width), 1)
    row = lax.broadcasted_iota(jnp.int32, (8, width), 0)
    unit = (lane == row).astype(F32)
    block_of = lax.broadcasted_iota(jnp.int32, (blocks, 8, width), 0)
    first_lanes = lax.broadcasted_iota(jnp.int32, (blocks, 8, width), 2) < 8

    def spread(value, i):
        return jnp.broadcast_to(value[i : i + 1, :], (8, width))

    def step(block, carry):
        start = pl.multiple_of(block * 8, 8)
        own = gram_ref[pl.ds(start, 8), :]
        column = [jnp.broadcast_to(own[:, m : m + 1], (8, width)) for m in range(8)]
        entry = [[spread(column[m], i) if m <= i else None for m in range(8)] for i in range(8)]
        replaced = jnp.where(lane < 8, unit, own)
        rows = [spread(replaced, i) for i in range(8)]
        inverse, solved = [], []
        for j in range(8):
            inverse.append(lax.rsqrt(entry[j][j]))
            solved.append(rows[j] * inverse[j])
            for i in range(j + 1, 8):
                entry[i][j] = entry[i][j] * inverse[j]
            for i in range(j + 1, 8):
                rows[i] = rows[i] - entry[i][j] * solved[j]
                for m in range(j + 1, i + 1):
                    entry[i][m] = entry[i][m] - entry[i][j] * entry[m][j]
        back = list(solved)
        for j in reversed(range(8)):
            for i in range(j + 1, 8):
                back[j] = back[j] - entry[i][j] * back[i]
            back[j] = back[j] * inverse[j]
        done = solved[0]
        for j in range(1, 8):
            done = jnp.where(row == j, solved[j], done)
        whole = gram_ref[...].reshape(blocks, 8, width)
        update = jnp.where(first_lanes, 0.0, whole)
        for m in range(8):
            update = update - whole[:, :, m : m + 1] * back[m][None]
        whole = jnp.where(block_of > block, update, jnp.where(block_of == block, done[None], whole))
        gram_ref[...] = pltpu.roll(whole.reshape(width, width), width - 8, 1)
        return carry

    lax.fori_loop(0, blocks, step, 0)
    lower = lax.broadcasted_iota(jnp.int32, (width, width), 0) >= lax.broadcasted_iota(
        jnp.int32, (width, width), 1
    )
    gram_ref[...] = jnp.where(lower, gram_ref[...], 0.0)


def kernel(
    n_cuts, n_rank, scale_left,
    one_ref, two_ref, sketch_ref, core_ref, left_ref, returned_ref, reduced_ref,
    one, two, sketch, core, one_high, one_low,
    bridge_part, bridge_swap, bridge_slices, bridge_half, bridge,
    first_rows, full_two, projected, second_rows, returned, gram,
    part, swapped, half, recv_rank, recv_slice, whole,
    load_sem, swap_send, swap_recv, slice_send, slice_recv, rank_send, rank_recv,
    two_send, two_recv, back_send, back_recv,
):
    slices, local, width = one_ref.shape
    out_width = sketch_ref.shape[1]
    band = out_width // n_rank
    small, half_width = local // 2, width // 2
    n_slices = n_cuts // 2
    side = math.isqrt(n_rank)
    side = side if side * side == n_rank else n_rank
    other = n_rank // side
    my_cut, my_rank = lax.axis_index("cuts"), lax.axis_index("rank")
    my_slice, my_core = lax.div(my_cut, 2), lax.rem(my_cut, 2)
    full, extra = slices // n_rank, slices % n_rank
    stride = max((n_rank - 1) // (extra - 1), 1) if extra > 1 else 1
    slots = full + (1 if extra else 0)

    def has_extra(rank):
        return jnp.logical_and(lax.rem(rank, stride) == 0, lax.div(rank, stride) < extra)

    def away(step, length):
        return min(step, length - step)

    partner = (my_cut + 1 - 2 * my_core, my_rank)
    slice_steps = sorted(range(1, n_slices), key=lambda k: -away(k, n_slices))
    slice_peers = [lax.rem(my_slice + k, n_slices) for k in slice_steps]
    rank_steps = sorted(
        ((i, j) for i in range(side) for j in range(other) if i or j),
        key=lambda t: -(away(t[0], side) + away(t[1], other)),
    )
    rank_peers = [
        lax.rem(lax.div(my_rank, other) + i, side) * other + lax.rem(lax.rem(my_rank, other) + j, other)
        for i, j in rank_steps
    ]

    def slice_device(peer):
        return (peer * 2 + my_core, my_rank)

    def rank_device(peer):
        return (my_cut, peer)

    def remote(source, target, send, recv, device):
        return pltpu.make_async_remote_copy(
            src_ref=source, dst_ref=target, send_sem=send, recv_sem=recv,
            device_id=device, device_id_type=MESH,
        )

    def rows_of(index, size):
        return pl.ds(pl.multiple_of(index * size, size), size)

    barrier = pltpu.get_barrier_semaphore()
    greeted = [partner] + [slice_device(p) for p in slice_peers] + [rank_device(p) for p in rank_peers]
    for device in greeted:
        pl.semaphore_signal(barrier, inc=1, device_id=device, device_id_type=MESH)
    loads = [
        pltpu.make_async_copy(source, target, load_sem.at[k])
        for k, (source, target) in enumerate(
            ((two_ref, two), (sketch_ref, sketch), (core_ref, core), (one_ref, one))
        )
    ]
    for load in loads:
        load.start()
    loads[0].wait()
    loads[1].wait()
    sketch_parts = split(sketch[...])
    sketched = product(split(two[...].reshape(slices * local, width)), sketch_parts, NN)
    loads[2].wait()
    lanes = jnp.concatenate([sketched[n * local : (n + 1) * local] for n in range(slices)], axis=1)
    weights = jnp.concatenate([core[n] for n in range(slices)], axis=1)
    bridge_part[...] = product(split(lanes), split(weights), NT)
    loads[3].wait()
    pl.semaphore_wait(barrier, len(greeted))

    pending = []

    def swap(source, target, phase):
        copy = remote(source, target, swap_send.at[phase], swap_recv.at[phase], partner)
        copy.start()
        pending.append(copy)
        return copy

    def send_slices(source, target, phase):
        for peer in slice_peers:
            copy = remote(source, target, slice_send.at[phase, peer], slice_recv.at[phase, my_slice], slice_device(peer))
            copy.start()
            pending.append(copy)

    def land_slices(target_of, phase):
        for peer in slice_peers:
            place = target_of(peer)
            remote(place, place, slice_send.at[phase, peer], slice_recv.at[phase, peer], slice_device(peer)).wait_recv()

    def send_rank(source_of, target, phase):
        for peer in rank_peers:
            copy = remote(source_of(peer), target, rank_send.at[phase, peer], rank_recv.at[phase, my_rank], rank_device(peer))
            copy.start()
            pending.append(copy)

    def land_rank(target_of, phase):
        for peer in rank_peers:
            place = target_of(peer)
            remote(place, place, rank_send.at[phase, peer], rank_recv.at[phase, peer], rank_device(peer)).wait_recv()

    def total(ref, count):
        value = ref[0]
        for k in range(1, count):
            value = value + ref[k]
        return value

    own_rows = rows_of(my_rank, local)

    def send_two(first, last):
        for peer in rank_peers[first:last]:
            for slot in range(full):
                n = slot * n_rank + peer
                copy = remote(two.at[n], full_two.at[slot, own_rows, :], two_send.at[n], two_recv.at[slot, my_rank], rank_device(peer))
                copy.start()
                pending.append(copy)

    def extra_two(i, action):
        n, target_rank = full * n_rank + i, i * stride

        @pl.when(my_rank != target_rank)
        def _():
            copy = remote(two.at[n], full_two.at[full, own_rows, :], two_send.at[n], two_recv.at[full, my_rank], (my_cut, target_rank))
            action(copy)

    def keep_two():
        for slot in range(full):
            full_two[slot, own_rows, :] = two[slot * n_rank + my_rank]
        for i in range(extra):
            @pl.when(my_rank == i * stride)
            def _():
                full_two[full, own_rows, :] = two[full * n_rank + i]

    def land_two():
        for slot in range(slots):
            def wait_rows():
                for peer in rank_peers:
                    place = full_two.at[slot, rows_of(peer, local), :]
                    remote(place, place, two_send.at[0], two_recv.at[slot, peer], rank_device(peer)).wait_recv()
            if slot < full:
                wait_rows()
            else:
                pl.when(has_extra(my_rank))(wait_rows)

    def pieces(k):
        count = len(rank_peers)
        cuts = [0] + [round(count * part) for part in PIECES] + [count]
        send_two(cuts[k], cuts[k + 1])
        if k == EXTRA_PIECE:
            for i in range(extra):
                extra_two(i, lambda copy: copy.start())

    away_rows = pl.ds(pl.multiple_of((1 - my_core) * small, small), small)
    step = swap(bridge_part.at[away_rows, :], bridge_swap, 0)
    pieces(0)
    keep_two()
    one_high[...], one_low[...] = split(one[...].reshape(slices * local, width))
    step.wait_recv()
    bridge_slices[my_slice] = bridge_part[rows_of(my_core, small), :] + bridge_swap[...]
    send_slices(bridge_slices.at[my_slice], bridge_slices.at[my_slice], 0)
    land_slices(lambda peer: bridge_slices.at[peer], 0)
    own = bridge_half.at[my_core, rows_of(my_rank, small), :]
    own[...] = total(bridge_slices, n_slices)
    send_rank(lambda peer: own, own, 0)
    pieces(1)
    land_rank(lambda peer: bridge_half.at[my_core, rows_of(peer, small), :], 0)
    swap(bridge_half.at[my_core], bridge_half.at[my_core], 1).wait_recv()
    for r in range(n_rank):
        for h in range(2):
            bridge[r * local + h * small : r * local + (h + 1) * small, :] = bridge_half[h, r * small : (r + 1) * small, :]

    def reduce(rows_bf, matrix_parts, index, between):
        both = product(rows_bf, matrix_parts, TN)
        for h in range(2):
            part[index, h] = both[:, h * half_width : (h + 1) * half_width]
        step = swap(part.at[index, 1 - my_core], swapped.at[index], 2 + 2 * index)
        between[0]()
        step.wait_recv()
        half[index] = part[index, my_core] + swapped[index]
        recv_rank[index, my_rank] = half[index, rows_of(my_rank, band), :]
        send_rank(lambda peer: half.at[index, rows_of(peer, band), :], recv_rank.at[index, my_rank], 1 + 2 * index)
        between[1]()
        land_rank(lambda peer: recv_rank.at[index, peer], 1 + 2 * index)
        recv_slice[index, my_slice] = total(recv_rank.at[index], n_rank)
        place = recv_slice.at[index, my_slice]
        send_slices(place, place, 1 + index)
        between[2]()
        land_slices(lambda peer: recv_slice.at[index, peer], 1 + index)
        own = whole.at[index, my_core, rows_of(my_rank, band), :]
        own[...] = total(recv_slice.at[index], n_slices)
        send_rank(lambda peer: own, own, 2 + 2 * index)
        between[3]()
        land_rank(lambda peer: whole.at[index, my_core, rows_of(peer, band), :], 2 + 2 * index)
        swap(whole.at[index, my_core], whole.at[index, my_core], 3 + 2 * index).wait_recv()
        return jnp.concatenate([whole[index, 0], whole[index, 1]], axis=1)

    def nothing():
        pass

    first_rows[...] = product((one_high[...], one_low[...]), split(bridge[...]), NN)
    first_sum = reduce(
        split(first_rows[...]), (one_high[...], one_low[...]), 0,
        (nothing, nothing, lambda: pieces(2), lambda: pieces(3)),
    )
    gram[...] = exact(first_sum, bridge[...], NN)
    inverse_factor(gram, out_width)
    first_carry = split(exact(gram[...], first_sum, NN))
    first_inverse = split(gram[...] * scale_left)
    land_two()

    for slot in range(slots):
        here = slice(slot * out_width, (slot + 1) * out_width)

        def project():
            block = product(first_carry, split(full_two[slot]), NN)
            projected[here, :] = block
            second_rows[here, :] = product(split(block), sketch_parts, NN)

        def blank():
            projected[here, :] = jnp.zeros((out_width, width), F32)
            second_rows[here, :] = jnp.zeros((out_width, out_width), F32)

        if slot < full:
            project()
        else:
            pl.when(has_extra(my_rank))(project)
            pl.when(jnp.logical_not(has_extra(my_rank)))(blank)

    def back(slot, peer):
        n = slot * n_rank + (my_rank if slot < full else lax.div(my_rank, stride))
        source = second_rows.at[pl.ds(pl.multiple_of(slot * out_width + peer * band, 8), band), :]
        return remote(source, returned.at[n], back_send.at[slot, peer], back_recv.at[n], rank_device(peer))

    def give_back():
        for slot in range(slots):
            n = slot * n_rank + (my_rank if slot < full else lax.div(my_rank, stride))

            def send_rows():
                returned[n] = second_rows[pl.ds(pl.multiple_of(slot * out_width + my_rank * band, 8), band), :]
                for peer in rank_peers:
                    back(slot, peer).start()
            if slot < full:
                send_rows()
            else:
                pl.when(has_extra(my_rank))(send_rows)

    def finish_left():
        ortho = product(split(first_rows[...]), first_inverse, NT)
        left_ref[...] = ortho.reshape(slices, local, out_width)

    def land_back():
        for n in range(slices):
            @pl.when(my_rank != (n % n_rank if n < full * n_rank else (n - full * n_rank) * stride))
            def _():
                remote(returned.at[n], returned.at[n], back_send.at[0, 0], back_recv.at[n], partner).wait_recv()
        returned_ref[...] = returned[...]

    reduced_ref[...] = reduce(
        split(second_rows[...]), split(projected[...]), 1, (nothing, nothing, give_back, finish_left),
    )
    land_back()

    for copy in pending:
        copy.wait_send()
    for i in range(extra):
        extra_two(i, lambda copy: copy.wait_send())
    for slot in range(slots):
        def sent():
            for peer in rank_peers:
                back(slot, peer).wait_send()
        if slot < full:
            sent()
        else:
            pl.when(has_extra(my_rank))(sent)


def finish_kernel(scale_middle, reduced_ref, sketch_ref, returned_ref, left_in_ref, left_ref, middle_ref, carry_ref, held, gram, sems):
    into = pltpu.make_async_copy(left_in_ref, held, sems.at[0])
    into.start()
    slices, band, out_width = returned_ref.shape
    gram[...] = exact(reduced_ref[...], sketch_ref[...], NN)
    into.wait()
    out = pltpu.make_async_copy(held, left_ref, sems.at[1])
    out.start()
    inverse_factor(gram, out_width)
    carry_ref[...] = exact(gram[...], reduced_ref[...], NN)
    flat = returned_ref[...].reshape(slices * band, out_width)
    middle = product(split(flat), split(gram[...] * scale_middle), NT)
    middle_ref[...] = middle.reshape(slices, band, out_width)
    out.wait()


def solution(mesh):
    n_cuts, n_rank = mesh.shape["cuts"], mesh.shape["rank"]

    def on_device(core_one, core_two, right_sketch, sketch_core):
        local, slices, width = core_one.shape
        out_width = right_sketch.shape[1]
        band, n_slices = out_width // n_rank, n_cuts // 2
        slots = -(-slices // n_rank)
        rows = local * slices
        scale_left = math.sqrt(local * n_rank * slices * n_cuts)
        scale_middle = math.sqrt(out_width * slices * n_cuts)
        vmem, sems = pltpu.VMEM, pltpu.SemaphoreType.DMA
        any_place, in_vmem = pl.BlockSpec(memory_space=pl.ANY), pl.BlockSpec(memory_space=pltpu.VMEM)
        left, returned, reduced = pl.pallas_call(
            functools.partial(kernel, n_cuts, n_rank, scale_left),
            out_shape=(
                jax.ShapeDtypeStruct((slices, local, out_width), F32),
                jax.ShapeDtypeStruct((slices, band, out_width), F32),
                jax.ShapeDtypeStruct((out_width, width), F32),
            ),
            in_specs=[any_place] * 4,
            out_specs=(in_vmem,) * 3,
            scratch_shapes=[
                vmem((slices, local, width), F32),
                vmem((slices, local, width), F32),
                vmem((width, out_width), F32),
                vmem((slices, out_width, out_width), F32),
                vmem((rows, width), BF16),
                vmem((rows, width), BF16),
                vmem((local, out_width), F32),
                vmem((local // 2, out_width), F32),
                vmem((n_slices, local // 2, out_width), F32),
                vmem((2, width // 2, out_width), F32),
                vmem((width, out_width), F32),
                vmem((rows, out_width), F32),
                vmem((slots, width, width), F32),
                vmem((slots * out_width, width), F32),
                vmem((slots * out_width, out_width), F32),
                vmem((slices, band, out_width), F32),
                vmem((out_width, out_width), F32),
                vmem((2, 2, out_width, width // 2), F32),
                vmem((2, out_width, width // 2), F32),
                vmem((2, out_width, width // 2), F32),
                vmem((2, n_rank, band, width // 2), F32),
                vmem((2, n_slices, band, width // 2), F32),
                vmem((2, 2, out_width, width // 2), F32),
                sems((4,)),
                sems((6,)),
                sems((6,)),
                sems((3, n_slices)),
                sems((3, n_slices)),
                sems((5, n_rank)),
                sems((5, n_rank)),
                sems((slices,)),
                sems((slots, n_rank)),
                sems((slots, n_rank)),
                sems((slices,)),
            ],
            compiler_params=pltpu.CompilerParams(
                collective_id=0, has_side_effects=True, vmem_limit_bytes=60 * 1024 * 1024
            ),
        )(
            core_one.transpose(1, 0, 2), core_two.transpose(1, 0, 2),
            right_sketch, sketch_core.transpose(1, 0, 2),
        )
        left, middle, carry = pl.pallas_call(
            functools.partial(finish_kernel, scale_middle),
            out_shape=(
                jax.ShapeDtypeStruct((slices, local, out_width), F32),
                jax.ShapeDtypeStruct((slices, band, out_width), F32),
                jax.ShapeDtypeStruct((out_width, width), F32),
            ),
            in_specs=[in_vmem] * 3 + [any_place],
            out_specs=(any_place, in_vmem, in_vmem),
            scratch_shapes=[vmem((slices, local, out_width), F32), vmem((out_width, out_width), F32), sems((2,))],
        )(reduced, right_sketch, returned, left)
        return left.transpose(1, 0, 2), middle.transpose(1, 0, 2), carry

    placed = (P("rank", "cuts", None), P("rank", "cuts", None), P(), P(None, "cuts", None))
    return jax.shard_map(
        on_device,
        mesh=mesh,
        in_specs=placed,
        out_specs=(P("rank", "cuts", None), P("rank", "cuts", None), P()),
        check_vma=False,
    )
```

time: 110 us -> 88.6 us (0.81)
  Pallas kernels: 104 us -> 87.8 us
  local copies, waits for them, and re-layouts: 4.91 us -> 0 us
    pallas_call x1 -> x2, Pallas kernels: 104 us -> 87.8 us  [the longest x1 79.2 us: on_device(): pl.pallas_call(functools.partial(kernel, n_cuts, n_rank, scale_left), out...]
    unnamed x3 -> x0, local copies, waits for them, and re-layouts: 4.91 us -> none
where the time goes in v1:
time: 88.6 us; the launch traced here: 88.4 us
  Pallas kernels  87.8 us (99%)
    pallas_call x1, Pallas kernels, on_device(): pl.pallas_call(functools.partial(kernel, n_cuts, n_rank, scale_left), out...  79.2 us
    pallas_call x1, Pallas kernels, on_device(): pl.pallas_call(functools.partial(finish_kernel, scale_middle), out_shape=...  8.62 us

profile of v1, /device:TPU:1, one launch (start us, length us, event | category | flops | bytes accessed | tf_op | source)
XLA Modules:
  0.0 88.4 jit_solution(7556507639611697561)
XLA Ops:
  0.6 79.2 %shard_map.67 = (f32[20,32,128]{2,1,0:T(8,128)}, f32[20,8,128]{2,1,0:T(8,128)}, f32[128,512]{1,0:T(8,128)}) custom-call(f32[20,32,512]{2,1,0:T(8,128)} %bitcast.5, f32[20,32,512]{2,1,0:T(8,128)} %bitcast.6, f32[512,128]{1,0:T(8,128)} %sketch_ref.3, f32[20,128,128]{2,1,0:T(8,128)} %bitcast.7), custom_call_target="tpu_custom_call" | custom-call | tf_op jit(solution)/shard_map/pallas_call | solution.py:403
  79.8 8.6 %shard_map.68 = (f32[20,32,128]{2,1,0:T(8,128)}, f32[20,8,128]{2,1,0:T(8,128)}, f32[128,512]{1,0:T(8,128)}) custom-call(f32[128,512]{1,0:T(8,128)} %get-tuple-element.9.reduced_ref, f32[512,128]{1,0:T(8,128)} %sketch_ref.3, f32[20,8,128]{2,1,0:T(8,128)} %get-tuple-element.10.returned_ref, f32[20,32,128]{2,1,0:T(8,128)} %get-tuple-element.11.left_in_ref), custom_call_target="tpu_custom_call" | custom-call | tf_op jit(solution)/shard_map/pallas_call | solution.py:455

commit v2 on v1

--- a/solution.py
+++ b/solution.py
@@ -14,7 +14,7 @@
 NN = (((1,), (0,)), ((), ()))
 NT = (((1,), (1,)), ((), ()))
 TN = (((0,), (0,)), ((), ()))
-PIECES = (0.25, 0.5, 0.7)
+PIECES = (0.35, 0.6, 0.8)
 EXTRA_PIECE = 3
 
 
@@ -35,24 +35,28 @@
     )
 
 
-def inverse_factor(gram_ref, width):
+def inverse_factor(gram_ref, rows_ref, columns_ref, width):
     blocks = width // 8
     lane = lax.broadcasted_iota(jnp.int32, (8, width), 1)
     row = lax.broadcasted_iota(jnp.int32, (8, width), 0)
-    unit = (lane == row).astype(F32)
-    block_of = lax.broadcasted_iota(jnp.int32, (blocks, 8, width), 0)
-    first_lanes = lax.broadcasted_iota(jnp.int32, (blocks, 8, width), 2) < 8
-
-    def spread(value, i):
-        return jnp.broadcast_to(value[i : i + 1, :], (8, width))
-
-    def step(block, carry):
-        start = pl.multiple_of(block * 8, 8)
-        own = gram_ref[pl.ds(start, 8), :]
-        column = [jnp.broadcast_to(own[:, m : m + 1], (8, width)) for m in range(8)]
-        entry = [[spread(column[m], i) if m <= i else None for m in range(8)] for i in range(8)]
-        replaced = jnp.where(lane < 8, unit, own)
-        rows = [spread(replaced, i) for i in range(8)]
+    rest = gram_ref[...].reshape(blocks, 8, width)
+    own, rest = rest[0], rest[1:]
+    for block in range(blocks):
+        base = 8 * block
+        last = block + 1 == blocks
+        inside = jnp.logical_and(lane >= base, lane < base + 8)
+        slot = (block % 2) * 8
+        for m in range(8):
+            columns_ref[(slot + m) * 8 : (slot + m + 1) * 8, :] = jnp.broadcast_to(own[:, base + m : base + m + 1], (8, width))
+        rows_ref[slot : slot + 8, :] = jnp.where(inside, (lane == row + base).astype(F32), own)
+        entry = [
+            [jnp.broadcast_to(columns_ref[(slot + m) * 8 + i : (slot + m) * 8 + i + 1, :], (8, width)) if m <= i else None for m in range(8)]
+            for i in range(8)
+        ]
+        rows = [jnp.broadcast_to(rows_ref[slot + i : slot + i + 1, :], (8, width)) for i in range(8)]
+        if not last:
+            ahead = [jnp.broadcast_to(rest[0][:, base + m : base + m + 1], (8, width)) for m in range(8)]
+            following = jnp.where(inside, 0.0, rest[0])
         inverse, solved = [], []
         for j in range(8):
             inverse.append(lax.rsqrt(entry[j][j]))
@@ -63,27 +67,29 @@
                 rows[i] = rows[i] - entry[i][j] * solved[j]
                 for m in range(j + 1, i + 1):
                     entry[i][m] = entry[i][m] - entry[i][j] * entry[m][j]
+            if not last:
+                factor = ahead[j] * inverse[j]
+                following = following - factor * solved[j]
+                for m in range(j + 1, 8):
+                    ahead[m] = ahead[m] - factor * entry[m][j]
+        done = solved[0]
+        for j in range(1, 8):
+            done = jnp.where(row == j, solved[j], done)
+        gram_ref[base : base + 8, :] = jnp.where(lane <= row + base, done, 0.0)
+        if last:
+            break
+        own, rest = following, rest[1:]
+        if block + 2 == blocks:
+            continue
         back = list(solved)
         for j in reversed(range(8)):
             for i in range(j + 1, 8):
                 back[j] = back[j] - entry[i][j] * back[i]
             back[j] = back[j] * inverse[j]
-        done = solved[0]
-        for j in range(1, 8):
-            done = jnp.where(row == j, solved[j], done)
-        whole = gram_ref[...].reshape(blocks, 8, width)
-        update = jnp.where(first_lanes, 0.0, whole)
+        update = jnp.where(inside[None], 0.0, rest)
         for m in range(8):
-            update = update - whole[:, :, m : m + 1] * back[m][None]
-        whole = jnp.where(block_of > block, update, jnp.where(block_of == block, done[None], whole))
-        gram_ref[...] = pltpu.roll(whole.reshape(width, width), width - 8, 1)
-        return carry
-
-    lax.fori_loop(0, blocks, step, 0)
-    lower = lax.broadcasted_iota(jnp.int32, (width, width), 0) >= lax.broadcasted_iota(
-        jnp.int32, (width, width), 1
-    )
-    gram_ref[...] = jnp.where(lower, gram_ref[...], 0.0)
+            update = update - rest[:, :, base + m : base + m + 1] * back[m][None]
+        rest = update
 
 
 def kernel(
@@ -91,7 +97,7 @@
     one_ref, two_ref, sketch_ref, core_ref, left_ref, returned_ref, reduced_ref,
     one, two, sketch, core, one_high, one_low,
     bridge_part, bridge_swap, bridge_slices, bridge_half, bridge,
-    first_rows, full_two, projected, second_rows, returned, gram,
+    first_rows, full_two, projected, second_rows, returned, gram, gram_rows, gram_columns,
     part, swapped, half, recv_rank, recv_slice, whole,
     load_sem, swap_send, swap_recv, slice_send, slice_recv, rank_send, rank_recv,
     two_send, two_recv, back_send, back_recv,
@@ -110,8 +116,17 @@
     stride = max((n_rank - 1) // (extra - 1), 1) if extra > 1 else 1
     slots = full + (1 if extra else 0)
 
+    square = extra == side and side == other
+
+    def extra_owner(i):
+        return i * other + lax.rem(i + 2 * my_core, other) if square else i * stride
+
+    def extra_held(rank):
+        return lax.div(rank, other if square else stride)
+
     def has_extra(rank):
-        return jnp.logical_and(lax.rem(rank, stride) == 0, lax.div(rank, stride) < extra)
+        held = extra_held(rank)
+        return jnp.logical_and(held < extra, rank == extra_owner(held))
 
     def away(step, length):
         return min(step, length - step)
@@ -213,7 +228,7 @@
                 pending.append(copy)
 
     def extra_two(i, action):
-        n, target_rank = full * n_rank + i, i * stride
+        n, target_rank = full * n_rank + i, extra_owner(i)
 
         @pl.when(my_rank != target_rank)
         def _():
@@ -224,7 +239,7 @@
         for slot in range(full):
             full_two[slot, own_rows, :] = two[slot * n_rank + my_rank]
         for i in range(extra):
-            @pl.when(my_rank == i * stride)
+            @pl.when(my_rank == extra_owner(i))
             def _():
                 full_two[full, own_rows, :] = two[full * n_rank + i]
 
@@ -300,7 +315,7 @@
         (nothing, nothing, lambda: pieces(2), lambda: pieces(3)),
     )
     gram[...] = exact(first_sum, bridge[...], NN)
-    inverse_factor(gram, out_width)
+    inverse_factor(gram, gram_rows, gram_columns, out_width)
     first_carry = split(exact(gram[...], first_sum, NN))
     first_inverse = split(gram[...] * scale_left)
     land_two()
@@ -324,13 +339,13 @@
             pl.when(jnp.logical_not(has_extra(my_rank)))(blank)
 
     def back(slot, peer):
-        n = slot * n_rank + (my_rank if slot < full else lax.div(my_rank, stride))
+        n = slot * n_rank + (my_rank if slot < full else extra_held(my_rank))
         source = second_rows.at[pl.ds(pl.multiple_of(slot * out_width + peer * band, 8), band), :]
         return remote(source, returned.at[n], back_send.at[slot, peer], back_recv.at[n], rank_device(peer))
 
     def give_back():
         for slot in range(slots):
-            n = slot * n_rank + (my_rank if slot < full else lax.div(my_rank, stride))
+            n = slot * n_rank + (my_rank if slot < full else extra_held(my_rank))
 
             def send_rows():
                 returned[n] = second_rows[pl.ds(pl.multiple_of(slot * out_width + my_rank * band, 8), band), :]
@@ -347,7 +362,7 @@
 
     def land_back():
         for n in range(slices):
-            @pl.when(my_rank != (n % n_rank if n < full * n_rank else (n - full * n_rank) * stride))
+            @pl.when(my_rank != (n % n_rank if n < full * n_rank else extra_owner(n - full * n_rank)))
             def _():
                 remote(returned.at[n], returned.at[n], back_send.at[0, 0], back_recv.at[n], partner).wait_recv()
         returned_ref[...] = returned[...]
@@ -371,7 +386,7 @@
             pl.when(has_extra(my_rank))(sent)
 
 
-def finish_kernel(scale_middle, reduced_ref, sketch_ref, returned_ref, left_in_ref, left_ref, middle_ref, carry_ref, held, gram, sems):
+def finish_kernel(scale_middle, reduced_ref, sketch_ref, returned_ref, left_in_ref, left_ref, middle_ref, carry_ref, held, gram, gram_rows, gram_columns, sems):
     into = pltpu.make_async_copy(left_in_ref, held, sems.at[0])
     into.start()
     slices, band, out_width = returned_ref.shape
@@ -379,7 +394,7 @@
     into.wait()
     out = pltpu.make_async_copy(held, left_ref, sems.at[1])
     out.start()
-    inverse_factor(gram, out_width)
+    inverse_factor(gram, gram_rows, gram_columns, out_width)
     carry_ref[...] = exact(gram[...], reduced_ref[...], NN)
     flat = returned_ref[...].reshape(slices * band, out_width)
     middle = product(split(flat), split(gram[...] * scale_middle), NT)
@@ -427,6 +442,8 @@
                 vmem((slots * out_width, out_width), F32),
                 vmem((slices, band, out_width), F32),
                 vmem((out_width, out_width), F32),
+                vmem((16, out_width), F32),
+                vmem((128, out_width), F32),
                 vmem((2, 2, out_width, width // 2), F32),
                 vmem((2, out_width, width // 2), F32),
                 vmem((2, out_width, width // 2), F32),
@@ -461,7 +478,7 @@
             ),
             in_specs=[in_vmem] * 3 + [any_place],
             out_specs=(any_place, in_vmem, in_vmem),
-            scratch_shapes=[vmem((slices, local, out_width), F32), vmem((out_width, out_width), F32), sems((2,))],
+            scratch_shapes=[vmem((slices, local, out_width), F32), vmem((out_width, out_width), F32), vmem((16, out_width), F32), vmem((128, out_width), F32), sems((2,))],
         )(reduced, right_sketch, returned, left)
         return left.transpose(1, 0, 2), middle.transpose(1, 0, 2), carry
 

time: 88.6 us -> 79.5 us (0.90)
  Pallas kernels: 87.8 us -> 78.5 us
    pallas_call x1, Pallas kernels: 79.2 us -> 71.9 us  [on_device(): pl.pallas_call(functools.partial(kernel, n_cuts, n_rank, scale_left), out...]
    pallas_call x1, Pallas kernels: 8.62 us -> 6.57 us  [on_device(): pl.pallas_call(functools.partial(finish_kernel, scale_middle), out_shape=...]
where the time goes in v2:
time: 79.5 us; the launch traced here: 79.3 us
  Pallas kernels  78.5 us (99%)
  between operations  0.8 us (1%)
    pallas_call x1, Pallas kernels, on_device(): pl.pallas_call(functools.partial(kernel, n_cuts, n_rank, scale_left), out...  71.9 us
    pallas_call x1, Pallas kernels, on_device(): pl.pallas_call(functools.partial(finish_kernel, scale_middle), out_shape=...  6.57 us

profile of v2, /device:TPU:1, one launch (start us, length us, event | category | flops | bytes accessed | tf_op | source)
XLA Modules:
  0.0 79.3 jit_solution(13132765353644596608)
XLA Ops:
  0.6 71.9 %shard_map.67 = (f32[20,32,128]{2,1,0:T(8,128)}, f32[20,8,128]{2,1,0:T(8,128)}, f32[128,512]{1,0:T(8,128)}) custom-call(f32[20,32,512]{2,1,0:T(8,128)} %bitcast.5, f32[20,32,512]{2,1,0:T(8,128)} %bitcast.6, f32[512,128]{1,0:T(8,128)} %sketch_ref.3, f32[20,128,128]{2,1,0:T(8,128)} %bitcast.7), custom_call_target="tpu_custom_call" | custom-call | tf_op jit(solution)/shard_map/pallas_call | solution.py:418
  72.6 6.6 %shard_map.68 = (f32[20,32,128]{2,1,0:T(8,128)}, f32[20,8,128]{2,1,0:T(8,128)}, f32[128,512]{1,0:T(8,128)}) custom-call(f32[128,512]{1,0:T(8,128)} %get-tuple-element.9.reduced_ref, f32[512,128]{1,0:T(8,128)} %sketch_ref.3, f32[20,8,128]{2,1,0:T(8,128)} %get-tuple-element.10.returned_ref, f32[20,32,128]{2,1,0:T(8,128)} %get-tuple-element.11.left_in_ref), custom_call_target="tpu_custom_call" | custom-call | tf_op jit(solution)/shard_map/pallas_call | solution.py:472

commit v3 on v2

--- a/solution.py
+++ b/solution.py
@@ -14,7 +14,7 @@
 NN = (((1,), (0,)), ((), ()))
 NT = (((1,), (1,)), ((), ()))
 TN = (((0,), (0,)), ((), ()))
-PIECES = (0.35, 0.6, 0.8)
+PIECES = (0.4, 0.6, 0.8)
 EXTRA_PIECE = 3
 
 
@@ -27,12 +27,6 @@
     (left_high, left_low), (right_high, right_low) = left, right
     dot = functools.partial(lax.dot_general, dimension_numbers=dims, preferred_element_type=F32)
     return dot(left_high, right_high) + (dot(left_high, right_low) + dot(left_low, right_high))
-
-
-def exact(left, right, dims):
-    return lax.dot_general(
-        left, right, dims, precision=lax.Precision.HIGHEST, preferred_element_type=F32
-    )
 
 
 def inverse_factor(gram_ref, rows_ref, columns_ref, width):
@@ -97,7 +91,7 @@
     one_ref, two_ref, sketch_ref, core_ref, left_ref, returned_ref, reduced_ref,
     one, two, sketch, core, one_high, one_low,
     bridge_part, bridge_swap, bridge_slices, bridge_half, bridge,
-    first_rows, full_two, projected, second_rows, returned, gram, gram_rows, gram_columns,
+    first_rows, full_two, second_rows, returned, left, gram, gram_rows, gram_columns,
     part, swapped, half, recv_rank, recv_slice, whole,
     load_sem, swap_send, swap_recv, slice_send, slice_recv, rank_send, rank_recv,
     two_send, two_recv, back_send, back_recv,
@@ -243,16 +237,10 @@
             def _():
                 full_two[full, own_rows, :] = two[full * n_rank + i]
 
-    def land_two():
-        for slot in range(slots):
-            def wait_rows():
-                for peer in rank_peers:
-                    place = full_two.at[slot, rows_of(peer, local), :]
-                    remote(place, place, two_send.at[0], two_recv.at[slot, peer], rank_device(peer)).wait_recv()
-            if slot < full:
-                wait_rows()
-            else:
-                pl.when(has_extra(my_rank))(wait_rows)
+    def land_two(slot):
+        for peer in rank_peers:
+            place = full_two.at[slot, rows_of(peer, local), :]
+            remote(place, place, two_send.at[0], two_recv.at[slot, peer], rank_device(peer)).wait_recv()
 
     def pieces(k):
         count = len(rank_peers)
@@ -281,10 +269,13 @@
         for h in range(2):
             bridge[r * local + h * small : r * local + (h + 1) * small, :] = bridge_half[h, r * small : (r + 1) * small, :]
 
-    def reduce(rows_bf, matrix_parts, index, between):
-        both = product(rows_bf, matrix_parts, TN)
+    def put_part(index, rows_parts, matrix_parts, first=True):
+        both = product(rows_parts, matrix_parts, TN)
         for h in range(2):
-            part[index, h] = both[:, h * half_width : (h + 1) * half_width]
+            piece = both[:, h * half_width : (h + 1) * half_width]
+            part[index, h] = piece if first else part[index, h] + piece
+
+    def reduce(index, between):
         step = swap(part.at[index, 1 - my_core], swapped.at[index], 2 + 2 * index)
         between[0]()
         step.wait_recv()
@@ -310,33 +301,28 @@
         pass
 
     first_rows[...] = product((one_high[...], one_low[...]), split(bridge[...]), NN)
-    first_sum = reduce(
-        split(first_rows[...]), (one_high[...], one_low[...]), 0,
-        (nothing, nothing, lambda: pieces(2), lambda: pieces(3)),
-    )
-    gram[...] = exact(first_sum, bridge[...], NN)
+    put_part(0, split(first_rows[...]), (one_high[...], one_low[...]))
+    first_sum = split(reduce(0, (nothing, nothing, lambda: pieces(2), lambda: pieces(3))))
+    gram[...] = product(first_sum, split(bridge[...]), NN)
     inverse_factor(gram, gram_rows, gram_columns, out_width)
-    first_carry = split(exact(gram[...], first_sum, NN))
+    first_carry = split(product(split(gram[...]), first_sum, NN))
     first_inverse = split(gram[...] * scale_left)
-    land_two()
 
     for slot in range(slots):
         here = slice(slot * out_width, (slot + 1) * out_width)
 
         def project():
+            land_two(slot)
             block = product(first_carry, split(full_two[slot]), NN)
-            projected[here, :] = block
-            second_rows[here, :] = product(split(block), sketch_parts, NN)
-
-        def blank():
-            projected[here, :] = jnp.zeros((out_width, width), F32)
-            second_rows[here, :] = jnp.zeros((out_width, out_width), F32)
+            parts = split(block)
+            rows = product(parts, sketch_parts, NN)
+            second_rows[here, :] = rows
+            put_part(1, split(rows), parts, slot == 0)
 
         if slot < full:
             project()
         else:
             pl.when(has_extra(my_rank))(project)
-            pl.when(jnp.logical_not(has_extra(my_rank)))(blank)
 
     def back(slot, peer):
         n = slot * n_rank + (my_rank if slot < full else extra_held(my_rank))
@@ -358,20 +344,29 @@
 
     def finish_left():
         ortho = product(split(first_rows[...]), first_inverse, NT)
-        left_ref[...] = ortho.reshape(slices, local, out_width)
+        left[...] = ortho.reshape(slices, local, out_width)
+        outs[0].start()
 
     def land_back():
         for n in range(slices):
             @pl.when(my_rank != (n % n_rank if n < full * n_rank else extra_owner(n - full * n_rank)))
             def _():
                 remote(returned.at[n], returned.at[n], back_send.at[0, 0], back_recv.at[n], partner).wait_recv()
-        returned_ref[...] = returned[...]
-
-    reduced_ref[...] = reduce(
-        split(second_rows[...]), split(projected[...]), 1, (nothing, nothing, give_back, finish_left),
-    )
-    land_back()
-
+        outs[1].start()
+
+    outs = [
+        pltpu.make_async_copy(source, target, load_sem.at[k])
+        for k, (source, target) in enumerate(((left, left_ref), (returned, returned_ref)))
+    ]
+
+    def land_and_finish():
+        land_back()
+        finish_left()
+
+    reduced_ref[...] = reduce(1, (nothing, nothing, give_back, land_and_finish))
+
+    for copy in outs:
+        copy.wait()
     for copy in pending:
         copy.wait_send()
     for i in range(extra):
@@ -386,17 +381,21 @@
             pl.when(has_extra(my_rank))(sent)
 
 
-def finish_kernel(scale_middle, reduced_ref, sketch_ref, returned_ref, left_in_ref, left_ref, middle_ref, carry_ref, held, gram, gram_rows, gram_columns, sems):
+def finish_kernel(scale_middle, reduced_ref, sketch_ref, returned_ref, left_in_ref, left_ref, middle_ref, carry_ref, held, rows, gram, gram_rows, gram_columns, sems):
     into = pltpu.make_async_copy(left_in_ref, held, sems.at[0])
     into.start()
+    rows_in = pltpu.make_async_copy(returned_ref, rows, sems.at[2])
+    rows_in.start()
     slices, band, out_width = returned_ref.shape
-    gram[...] = exact(reduced_ref[...], sketch_ref[...], NN)
+    reduced = split(reduced_ref[...])
+    gram[...] = product(reduced, split(sketch_ref[...]), NN)
     into.wait()
     out = pltpu.make_async_copy(held, left_ref, sems.at[1])
     out.start()
     inverse_factor(gram, gram_rows, gram_columns, out_width)
-    carry_ref[...] = exact(gram[...], reduced_ref[...], NN)
-    flat = returned_ref[...].reshape(slices * band, out_width)
+    carry_ref[...] = product(split(gram[...]), reduced, NN)
+    rows_in.wait()
+    flat = rows[...].reshape(slices * band, out_width)
     middle = product(split(flat), split(gram[...] * scale_middle), NT)
     middle_ref[...] = middle.reshape(slices, band, out_width)
     out.wait()
@@ -423,7 +422,7 @@
                 jax.ShapeDtypeStruct((out_width, width), F32),
             ),
             in_specs=[any_place] * 4,
-            out_specs=(in_vmem,) * 3,
+            out_specs=(any_place, any_place, in_vmem),
             scratch_shapes=[
                 vmem((slices, local, width), F32),
                 vmem((slices, local, width), F32),
@@ -438,9 +437,9 @@
                 vmem((width, out_width), F32),
                 vmem((rows, out_width), F32),
                 vmem((slots, width, width), F32),
-                vmem((slots * out_width, width), F32),
                 vmem((slots * out_width, out_width), F32),
                 vmem((slices, band, out_width), F32),
+                vmem((slices, local, out_width), F32),
                 vmem((out_width, out_width), F32),
                 vmem((16, out_width), F32),
                 vmem((128, out_width), F32),
@@ -476,9 +475,16 @@
                 jax.ShapeDtypeStruct((slices, band, out_width), F32),
                 jax.ShapeDtypeStruct((out_width, width), F32),
             ),
-            in_specs=[in_vmem] * 3 + [any_place],
+            in_specs=[in_vmem] * 2 + [any_place] * 2,
             out_specs=(any_place, in_vmem, in_vmem),
-            scratch_shapes=[vmem((slices, local, out_width), F32), vmem((out_width, out_width), F32), vmem((16, out_width), F32), vmem((128, out_width), F32), sems((2,))],
+            scratch_shapes=[
+                vmem((slices, local, out_width), F32),
+                vmem((slices, band, out_width), F32),
+                vmem((out_width, out_width), F32),
+                vmem((16, out_width), F32),
+                vmem((128, out_width), F32),
+                sems((3,)),
+            ],
         )(reduced, right_sketch, returned, left)
         return left.transpose(1, 0, 2), middle.transpose(1, 0, 2), carry
 

time: 79.5 us -> 78.5 us (0.987)
  no operation moved by 1% of the time
where the time goes in v3:
time: 78.5 us; the launch traced here: 78.4 us
  Pallas kernels  77.8 us (99%)
    pallas_call x1, Pallas kernels, on_device(): pl.pallas_call(functools.partial(kernel, n_cuts, n_rank, scale_left), out...  71.3 us
    pallas_call x1, Pallas kernels, on_device(): pl.pallas_call(functools.partial(finish_kernel, scale_middle), out_shape=...  6.46 us

profile of v3, /device:TPU:1, one launch (start us, length us, event | category | flops | bytes accessed | tf_op | source)
XLA Modules:
  0.0 78.4 jit_solution(4362597432593805489)
XLA Ops:
  0.6 71.3 %shard_map.67 = (f32[20,32,128]{2,1,0:T(8,128)}, f32[20,8,128]{2,1,0:T(8,128)}, f32[128,512]{1,0:T(8,128)}) custom-call(f32[20,32,512]{2,1,0:T(8,128)} %bitcast.5, f32[20,32,512]{2,1,0:T(8,128)} %bitcast.6, f32[512,128]{1,0:T(8,128)} %sketch_ref.3, f32[20,128,128]{2,1,0:T(8,128)} %bitcast.7), custom_call_target="tpu_custom_call" | custom-call | tf_op jit(solution)/shard_map/pallas_call | solution.py:417
  71.9 6.5 %shard_map.68 = (f32[20,32,128]{2,1,0:T(8,128)}, f32[20,8,128]{2,1,0:T(8,128)}, f32[128,512]{1,0:T(8,128)}) custom-call(f32[128,512]{1,0:T(8,128)} %get-tuple-element.9.reduced_ref, f32[512,128]{1,0:T(8,128)} %sketch_ref.3, f32[20,8,128]{2,1,0:T(8,128)} %get-tuple-element.10.returned_ref, f32[20,32,128]{2,1,0:T(8,128)} %get-tuple-element.11.left_in_ref), custom_call_target="tpu_custom_call" | custom-call | tf_op jit(solution)/shard_map/pallas_call | solution.py:471

commit v4 on v3

--- a/solution.py
+++ b/solution.py
@@ -88,8 +88,8 @@
 
 def kernel(
     n_cuts, n_rank, scale_left,
-    one_ref, two_ref, sketch_ref, core_ref, left_ref, returned_ref, reduced_ref,
-    one, two, sketch, core, one_high, one_low,
+    one_ref, two_ref, sketch_ref, core_ref, left_ref, returned_ref, reduced_ref, gram_ref,
+    one, two, sketch, core, one_high, one_low, square_high, square_low,
     bridge_part, bridge_swap, bridge_slices, bridge_half, bridge,
     first_rows, full_two, second_rows, returned, left, gram, gram_rows, gram_columns,
     part, swapped, half, recv_rank, recv_slice, whole,
@@ -254,10 +254,12 @@
     step = swap(bridge_part.at[away_rows, :], bridge_swap, 0)
     pieces(0)
     keep_two()
-    one_high[...], one_low[...] = split(one[...].reshape(slices * local, width))
     step.wait_recv()
     bridge_slices[my_slice] = bridge_part[rows_of(my_core, small), :] + bridge_swap[...]
     send_slices(bridge_slices.at[my_slice], bridge_slices.at[my_slice], 0)
+    one_high[...], one_low[...] = split(one[...].reshape(slices * local, width))
+    one_parts = (one_high[...], one_low[...])
+    square_high[...], square_low[...] = split(product(one_parts, one_parts, TN))
     land_slices(lambda peer: bridge_slices.at[peer], 0)
     own = bridge_half.at[my_core, rows_of(my_rank, small), :]
     own[...] = total(bridge_slices, n_slices)
@@ -300,9 +302,11 @@
     def nothing():
         pass
 
-    first_rows[...] = product((one_high[...], one_low[...]), split(bridge[...]), NN)
-    put_part(0, split(first_rows[...]), (one_high[...], one_low[...]))
-    first_sum = split(reduce(0, (nothing, nothing, lambda: pieces(2), lambda: pieces(3))))
+    def rows_one():
+        first_rows[...] = product((one_high[...], one_low[...]), split(bridge[...]), NN)
+
+    put_part(0, split(bridge[...]), (square_high[...], square_low[...]))
+    first_sum = split(reduce(0, (nothing, rows_one, lambda: pieces(2), lambda: pieces(3))))
     gram[...] = product(first_sum, split(bridge[...]), NN)
     inverse_factor(gram, gram_rows, gram_columns, out_width)
     first_carry = split(product(split(gram[...]), first_sum, NN))
@@ -363,7 +367,10 @@
         land_back()
         finish_left()
 
-    reduced_ref[...] = reduce(1, (nothing, nothing, give_back, land_and_finish))
+    second_sum = reduce(1, (nothing, nothing, give_back, land_and_finish))
+    outs.append(pltpu.make_async_copy(whole.at[1], reduced_ref, load_sem.at[2]))
+    outs[2].start()
+    gram_ref[...] = product(split(second_sum), sketch_parts, NN)
 
     for copy in outs:
         copy.wait()
@@ -381,20 +388,26 @@
             pl.when(has_extra(my_rank))(sent)
 
 
-def finish_kernel(scale_middle, reduced_ref, sketch_ref, returned_ref, left_in_ref, left_ref, middle_ref, carry_ref, held, rows, gram, gram_rows, gram_columns, sems):
-    into = pltpu.make_async_copy(left_in_ref, held, sems.at[0])
-    into.start()
-    rows_in = pltpu.make_async_copy(returned_ref, rows, sems.at[2])
-    rows_in.start()
-    slices, band, out_width = returned_ref.shape
-    reduced = split(reduced_ref[...])
-    gram[...] = product(reduced, split(sketch_ref[...]), NN)
-    into.wait()
-    out = pltpu.make_async_copy(held, left_ref, sems.at[1])
+def finish_kernel(
+    scale_middle, gram_ref, reduced_ref, returned_ref, left_in_ref, left_ref, middle_ref, carry_ref,
+    reduced, rows, held, gram, gram_rows, gram_columns, sems,
+):
+    loads = [
+        pltpu.make_async_copy(source, target, sems.at[k])
+        for k, (source, target) in enumerate(((left_in_ref, held), (returned_ref, rows), (reduced_ref, reduced)))
+    ]
+    for load in loads:
+        load.start()
+    slices, band, out_width = rows.shape
+    gram[...] = gram_ref[...]
+    inverse_factor(gram, gram_rows, gram_columns, out_width)
+    loads[0].wait()
+    out = pltpu.make_async_copy(held, left_ref, sems.at[3])
     out.start()
-    inverse_factor(gram, gram_rows, gram_columns, out_width)
-    carry_ref[...] = product(split(gram[...]), reduced, NN)
-    rows_in.wait()
+    inverse = split(gram[...])
+    loads[2].wait()
+    carry_ref[...] = product(inverse, split(jnp.concatenate([reduced[0], reduced[1]], axis=1)), NN)
+    loads[1].wait()
     flat = rows[...].reshape(slices * band, out_width)
     middle = product(split(flat), split(gram[...] * scale_middle), NT)
     middle_ref[...] = middle.reshape(slices, band, out_width)
@@ -414,15 +427,16 @@
         scale_middle = math.sqrt(out_width * slices * n_cuts)
         vmem, sems = pltpu.VMEM, pltpu.SemaphoreType.DMA
         any_place, in_vmem = pl.BlockSpec(memory_space=pl.ANY), pl.BlockSpec(memory_space=pltpu.VMEM)
-        left, returned, reduced = pl.pallas_call(
+        left, returned, reduced, gram = pl.pallas_call(
             functools.partial(kernel, n_cuts, n_rank, scale_left),
             out_shape=(
                 jax.ShapeDtypeStruct((slices, local, out_width), F32),
                 jax.ShapeDtypeStruct((slices, band, out_width), F32),
-                jax.ShapeDtypeStruct((out_width, width), F32),
+                jax.ShapeDtypeStruct((2, out_width, width // 2), F32),
+                jax.ShapeDtypeStruct((out_width, out_width), F32),
             ),
             in_specs=[any_place] * 4,
-            out_specs=(any_place, any_place, in_vmem),
+            out_specs=(any_place,) * 3 + (in_vmem,),
             scratch_shapes=[
                 vmem((slices, local, width), F32),
                 vmem((slices, local, width), F32),
@@ -430,6 +444,8 @@
                 vmem((slices, out_width, out_width), F32),
                 vmem((rows, width), BF16),
                 vmem((rows, width), BF16),
+                vmem((width, width), BF16),
+                vmem((width, width), BF16),
                 vmem((local, out_width), F32),
                 vmem((local // 2, out_width), F32),
                 vmem((n_slices, local // 2, out_width), F32),
@@ -475,17 +491,18 @@
                 jax.ShapeDtypeStruct((slices, band, out_width), F32),
                 jax.ShapeDtypeStruct((out_width, width), F32),
             ),
-            in_specs=[in_vmem] * 2 + [any_place] * 2,
+            in_specs=[in_vmem] + [any_place] * 3,
             out_specs=(any_place, in_vmem, in_vmem),
             scratch_shapes=[
+                vmem((2, out_width, width // 2), F32),
+                vmem((slices, band, out_width), F32),
                 vmem((slices, local, out_width), F32),
-                vmem((slices, band, out_width), F32),
                 vmem((out_width, out_width), F32),
                 vmem((16, out_width), F32),
                 vmem((128, out_width), F32),
-                sems((3,)),
+                sems((4,)),
             ],
-        )(reduced, right_sketch, returned, left)
+        )(gram, reduced, returned, left)
         return left.transpose(1, 0, 2), middle.transpose(1, 0, 2), carry
 
     placed = (P("rank", "cuts", None), P("rank", "cuts", None), P(), P(None, "cuts", None))

time: 78.5 us -> 77.1 us (0.982)
  Pallas kernels: 77.8 us -> 76.2 us
    pallas_call x1, Pallas kernels: 6.46 us -> 5.52 us  [on_device(): pl.pallas_call(functools.partial(finish_kernel, scale_middle), out_shape=...]
where the time goes in v4:
time: 77.1 us; the launch traced here: 77 us
  Pallas kernels  76.2 us (99%)
  between operations  0.8 us (1%)
    pallas_call x1, Pallas kernels, on_device(): pl.pallas_call(functools.partial(kernel, n_cuts, n_rank, scale_left), out...  70.7 us
    pallas_call x1, Pallas kernels, on_device(): pl.pallas_call(functools.partial(finish_kernel, scale_middle), out_shape=...  5.52 us

profile of v4, /device:TPU:1, one launch (start us, length us, event | category | flops | bytes accessed | tf_op | source)
XLA Modules:
  0.0 77.0 jit_solution(1610264555614594975)
XLA Ops:
  0.6 70.7 %shard_map.67 = (f32[20,32,128]{2,1,0:T(8,128)}, f32[20,8,128]{2,1,0:T(8,128)}, f32[2,128,256]{2,1,0:T(8,128)}, f32[128,128]{1,0:T(8,128)}) custom-call(f32[20,32,512]{2,1,0:T(8,128)} %bitcast.5, f32[20,32,512]{2,1,0:T(8,128)} %bitcast.6, f32[512,128]{1,0:T(8,128)} %sketch_ref.1, f32[20,128,128]{2,1,0:T(8,128)} %bitcast.7), custom_call_target="tpu_custom_call" | custom-call | tf_op jit(solution)/shard_map/pallas_call | solution.py:430
  71.3 5.5 %shard_map.68 = (f32[20,32,128]{2,1,0:T(8,128)}, f32[20,8,128]{2,1,0:T(8,128)}, f32[128,512]{1,0:T(8,128)}) custom-call(f32[128,128]{1,0:T(8,128)} %get-tuple-element.10.gram_ref, f32[2,128,256]{2,1,0:T(8,128)} %get-tuple-element.11.reduced_ref, f32[20,8,128]{2,1,0:T(8,128)} %get-tuple-element.12.returned_ref, f32[20,32,128]{2,1,0:T(8,128)} %get-tuple-element.13.left_in_ref), custom_call_target="tpu_custom_call" | custom-call | tf_op jit(solution)/shard_map/pallas_call | solution.py:487

commit v5 on v4

--- a/solution.py
+++ b/solution.py
@@ -264,8 +264,8 @@
     own = bridge_half.at[my_core, rows_of(my_rank, small), :]
     own[...] = total(bridge_slices, n_slices)
     send_rank(lambda peer: own, own, 0)
+    land_rank(lambda peer: bridge_half.at[my_core, rows_of(peer, small), :], 0)
     pieces(1)
-    land_rank(lambda peer: bridge_half.at[my_core, rows_of(peer, small), :], 0)
     swap(bridge_half.at[my_core], bridge_half.at[my_core], 1).wait_recv()
     for r in range(n_rank):
         for h in range(2):
@@ -293,10 +293,15 @@
         land_slices(lambda peer: recv_slice.at[index, peer], 1 + index)
         own = whole.at[index, my_core, rows_of(my_rank, band), :]
         own[...] = total(recv_slice.at[index], n_slices)
+        earlier = list(pending)
+        pending.clear()
         send_rank(lambda peer: own, own, 2 + 2 * index)
         between[3]()
+        for copy in earlier:
+            copy.wait_send()
         land_rank(lambda peer: whole.at[index, my_core, rows_of(peer, band), :], 2 + 2 * index)
-        swap(whole.at[index, my_core], whole.at[index, my_core], 3 + 2 * index).wait_recv()
+        step = swap(whole.at[index, my_core], whole.at[index, my_core], 3 + 2 * index)
+        step.wait_recv()
         return jnp.concatenate([whole[index, 0], whole[index, 1]], axis=1)
 
     def nothing():
@@ -366,26 +371,26 @@
     def land_and_finish():
         land_back()
         finish_left()
+        for i in range(extra):
+            extra_two(i, lambda copy: copy.wait_send())
+        for slot in range(slots):
+            def sent():
+                for peer in rank_peers:
+                    back(slot, peer).wait_send()
+            if slot < full:
+                sent()
+            else:
+                pl.when(has_extra(my_rank))(sent)
 
     second_sum = reduce(1, (nothing, nothing, give_back, land_and_finish))
     outs.append(pltpu.make_async_copy(whole.at[1], reduced_ref, load_sem.at[2]))
     outs[2].start()
     gram_ref[...] = product(split(second_sum), sketch_parts, NN)
 
+    for copy in pending:
+        copy.wait_send()
     for copy in outs:
         copy.wait()
-    for copy in pending:
-        copy.wait_send()
-    for i in range(extra):
-        extra_two(i, lambda copy: copy.wait_send())
-    for slot in range(slots):
-        def sent():
-            for peer in rank_peers:
-                back(slot, peer).wait_send()
-        if slot < full:
-            sent()
-        else:
-            pl.when(has_extra(my_rank))(sent)
 
 
 def finish_kernel(

time: 77.1 us -> 77 us (level)
  no operation moved by 1% of the time
where the time goes in v5:
time: 77 us; the launch traced here: 76.9 us
  Pallas kernels  76.1 us (99%)
  between operations  0.8 us (1%)
    pallas_call x1, Pallas kernels, on_device(): pl.pallas_call(functools.partial(kernel, n_cuts, n_rank, scale_left), out...  70.6 us
    pallas_call x1, Pallas kernels, on_device(): pl.pallas_call(functools.partial(finish_kernel, scale_middle), out_shape=...  5.52 us

profile of v5, /device:TPU:1, one launch (start us, length us, event | category | flops | bytes accessed | tf_op | source)
XLA Modules:
  0.0 76.9 jit_solution(11391779057132134860)
XLA Ops:
  0.6 70.6 %shard_map.67 = (f32[20,32,128]{2,1,0:T(8,128)}, f32[20,8,128]{2,1,0:T(8,128)}, f32[2,128,256]{2,1,0:T(8,128)}, f32[128,128]{1,0:T(8,128)}) custom-call(f32[20,32,512]{2,1,0:T(8,128)} %bitcast.5, f32[20,32,512]{2,1,0:T(8,128)} %bitcast.6, f32[512,128]{1,0:T(8,128)} %sketch_ref.1, f32[20,128,128]{2,1,0:T(8,128)} %bitcast.7), custom_call_target="tpu_custom_call" | custom-call | tf_op jit(solution)/shard_map/pallas_call | solution.py:435
  71.2 5.5 %shard_map.68 = (f32[20,32,128]{2,1,0:T(8,128)}, f32[20,8,128]{2,1,0:T(8,128)}, f32[128,512]{1,0:T(8,128)}) custom-call(f32[128,128]{1,0:T(8,128)} %get-tuple-element.10.gram_ref, f32[2,128,256]{2,1,0:T(8,128)} %get-tuple-element.11.reduced_ref, f32[20,8,128]{2,1,0:T(8,128)} %get-tuple-element.12.returned_ref, f32[20,32,128]{2,1,0:T(8,128)} %get-tuple-element.13.left_in_ref), custom_call_target="tpu_custom_call" | custom-call | tf_op jit(solution)/shard_map/pallas_call | solution.py:492

commit v6 on v5

--- a/solution.py
+++ b/solution.py
@@ -14,8 +14,8 @@
 NN = (((1,), (0,)), ((), ()))
 NT = (((1,), (1,)), ((), ()))
 TN = (((0,), (0,)), ((), ()))
-PIECES = (0.4, 0.6, 0.8)
-EXTRA_PIECE = 3
+PIECES = (0.4, 0.4, 0.6667)
+EXTRA_PIECE = 1
 
 
 def split(value):
@@ -277,7 +277,10 @@
             piece = both[:, h * half_width : (h + 1) * half_width]
             part[index, h] = piece if first else part[index, h] + piece
 
-    def reduce(index, between):
+    def reduce(index, right_ref, between):
+        def half_gram(core):
+            return product(split(whole[index, core]), split(right_ref[rows_of(core, half_width), :]), NN)
+
         step = swap(part.at[index, 1 - my_core], swapped.at[index], 2 + 2 * index)
         between[0]()
         step.wait_recv()
@@ -301,8 +304,9 @@
             copy.wait_send()
         land_rank(lambda peer: whole.at[index, my_core, rows_of(peer, band), :], 2 + 2 * index)
         step = swap(whole.at[index, my_core], whole.at[index, my_core], 3 + 2 * index)
+        own_gram = half_gram(my_core)
         step.wait_recv()
-        return jnp.concatenate([whole[index, 0], whole[index, 1]], axis=1)
+        return own_gram + half_gram(1 - my_core), jnp.concatenate([whole[index, 0], whole[index, 1]], axis=1)
 
     def nothing():
         pass
@@ -311,8 +315,8 @@
         first_rows[...] = product((one_high[...], one_low[...]), split(bridge[...]), NN)
 
     put_part(0, split(bridge[...]), (square_high[...], square_low[...]))
-    first_sum = split(reduce(0, (nothing, rows_one, lambda: pieces(2), lambda: pieces(3))))
-    gram[...] = product(first_sum, split(bridge[...]), NN)
+    gram[...], first_sum = reduce(0, bridge, (nothing, rows_one, lambda: pieces(2), lambda: pieces(3)))
+    first_sum = split(first_sum)
     inverse_factor(gram, gram_rows, gram_columns, out_width)
     first_carry = split(product(split(gram[...]), first_sum, NN))
     first_inverse = split(gram[...] * scale_left)
@@ -382,10 +386,9 @@
             else:
                 pl.when(has_extra(my_rank))(sent)
 
-    second_sum = reduce(1, (nothing, nothing, give_back, land_and_finish))
+    gram_ref[...], _ = reduce(1, sketch, (nothing, nothing, give_back, land_and_finish))
     outs.append(pltpu.make_async_copy(whole.at[1], reduced_ref, load_sem.at[2]))
     outs[2].start()
-    gram_ref[...] = product(split(second_sum), sketch_parts, NN)
 
     for copy in pending:
         copy.wait_send()

time: 77 us -> 75.1 us (0.975)
  Pallas kernels: 76.1 us -> 74.1 us
    pallas_call x1, Pallas kernels: 70.6 us -> 68.6 us  [on_device(): pl.pallas_call(functools.partial(kernel, n_cuts, n_rank, scale_left), out...]
where the time goes in v6:
time: 75.1 us; the launch traced here: 74.9 us
  Pallas kernels  74.1 us (99%)
  between operations  0.8 us (1%)
    pallas_call x1, Pallas kernels, on_device(): pl.pallas_call(functools.partial(kernel, n_cuts, n_rank, scale_left), out...  68.6 us
    pallas_call x1, Pallas kernels, on_device(): pl.pallas_call(functools.partial(finish_kernel, scale_middle), out_shape=...  5.52 us

profile of v6, /device:TPU:1, one launch (start us, length us, event | category | flops | bytes accessed | tf_op | source)
XLA Modules:
  0.0 74.9 jit_solution(5676590768567162489)
XLA Ops:
  0.6 68.6 %shard_map.67 = (f32[20,32,128]{2,1,0:T(8,128)}, f32[20,8,128]{2,1,0:T(8,128)}, f32[2,128,256]{2,1,0:T(8,128)}, f32[128,128]{1,0:T(8,128)}) custom-call(f32[20,32,512]{2,1,0:T(8,128)} %bitcast.5, f32[20,32,512]{2,1,0:T(8,128)} %bitcast.6, f32[512,128]{1,0:T(8,128)} %sketch_ref.1, f32[20,128,128]{2,1,0:T(8,128)} %bitcast.7), custom_call_target="tpu_custom_call" | custom-call | tf_op jit(solution)/shard_map/pallas_call | solution.py:438
  69.2 5.5 %shard_map.68 = (f32[20,32,128]{2,1,0:T(8,128)}, f32[20,8,128]{2,1,0:T(8,128)}, f32[128,512]{1,0:T(8,128)}) custom-call(f32[128,128]{1,0:T(8,128)} %get-tuple-element.10.gram_ref, f32[2,128,256]{2,1,0:T(8,128)} %get-tuple-element.11.reduced_ref, f32[20,8,128]{2,1,0:T(8,128)} %get-tuple-element.12.returned_ref, f32[20,32,128]{2,1,0:T(8,128)} %get-tuple-element.13.left_in_ref), custom_call_target="tpu_custom_call" | custom-call | tf_op jit(solution)/shard_map/pallas_call | solution.py:495
